TPU v7x, 256 devices: a whole 4x4x8 slice. The times are simulated.
256 devices in a mesh: rows: 128 (over z_hi, y, x, core), feat: 2 (over z_lo).
Axes of the slice: x: 4, y: 4, z: 8 (z_hi: 4, z_lo: 2; z = z_hi * 2 + z_lo), core: 2. Of those that a mesh axis runs over, the one named last changes fastest.
Arguments:
- features: bfloat16 [98304, 8192], P('rows', 'feat'), may hold values from -400 to 400
- group_index_list: int32 [98304], P('rows'), may hold values from 0 to 4095
- threshold_codes: int32 [98304], P('rows'), may hold values from 0 to 3
Outputs:
- counts: float32 [2, 98304], P(None, 'rows')
All inputs are finite; a program needn't handle non-finite values.
Results may differ from a plain program's by a relative error of at most 0.00058.
The roundings to bfloat16 on the way count: a program that leaves them out, or rounds other values in their place, can miss the bound.
Values may be sent and summed in bfloat16 or wider, within the bound.
A program may use at most 64 MiB of HBM per device.

v0:
```python
import math

import jax
import jax.numpy as jnp
from jax import lax
from jax.sharding import PartitionSpec as P

MEET = 3


SOFTNESS_FACTOR = 0.02


def from_behind(value, axis, steps):
    count = lax.axis_size(axis)
    pairs = [(source, (source + steps) % count) for source in range(count)]
    return lax.ppermute(value, axis, pairs)


def count_rows(score_matrix, level_codes, own_groups, other_groups):
    cutoff_levels = 0.2 + 0.15 * level_codes.astype(jnp.float32)
    weight_factors = jax.nn.sigmoid((score_matrix - cutoff_levels[:, None]) / SOFTNESS_FACTOR)
    same_group = own_groups[:, None] == other_groups[None, :]
    matched = jnp.sum(jnp.where(same_group, weight_factors, 0.0), axis=1)
    overall = jnp.sum(weight_factors, axis=1)
    return jnp.stack([matched, overall - matched])


def count_columns(score_matrix, level_codes, own_groups, other_groups):
    cutoff_levels = 0.2 + 0.15 * level_codes.astype(jnp.float32)
    weight_factors = jax.nn.sigmoid((score_matrix - cutoff_levels[None, :]) / SOFTNESS_FACTOR)
    same_group = other_groups[:, None] == own_groups[None, :]
    matched = jnp.sum(jnp.where(same_group, weight_factors, 0.0), axis=0)
    overall = jnp.sum(weight_factors, axis=0)
    return jnp.stack([matched, overall - matched])


def local(features, group_index_list, threshold_codes):
    rows_dev = features.shape[0]
    full_width = features.shape[1] * lax.axis_size("feat")
    widened = features.astype(jnp.float32)
    squares = lax.psum(jnp.sum(widened * widened, axis=1), "feat")
    inverse = lax.rsqrt(squares / full_width + 1e-06) / math.sqrt(full_width)
    normed = (widened * inverse[:, None]).astype(jnp.bfloat16)
    labels = jnp.stack([group_index_list, threshold_codes])
    counts = jnp.zeros((2, rows_dev), jnp.float32)
    for offset in range(1, MEET + 1):
        partner, partner_labels = from_behind((normed, labels), "rows", -offset)
        partial_value = lax.dot_general(
            normed, partner, (((1,), (1,)), ((), ())), preferred_element_type=jnp.float32
        )
        score_matrix = lax.psum(partial_value, "feat")
        counts = counts + count_rows(
            score_matrix, threshold_codes, group_index_list, partner_labels[0]
        )
        returned, sender_groups = from_behind((score_matrix, group_index_list), "rows", offset)
        counts = counts + count_columns(returned, threshold_codes, group_index_list, sender_groups)
    return counts


def solution(mesh):
    placed = (P("rows", "feat"), P("rows"), P("rows"))
    return jax.shard_map(
        local, mesh=mesh, in_specs=placed, out_specs=P(None, "rows"), check_vma=False
    )
```

profile of v0, /device:TPU:32, one launch (start us, length us, event | category | flops | bytes accessed | tf_op | source)
XLA Modules:
  0.0 1170.9 jit_solution(14858275859539918193)
XLA Ops:
  6.5 0.0 all-reduce.3.cloned.1.call-start
  6.5 4.1 fusion
  10.6 4.9 psum.28
  15.6 4.8 fusion.1
  20.4 10.1 collective-permute-start.5
  30.5 0.0 collective-permute-start.9
  30.5 1.1 collective-permute-start.1
  31.6 286.0 %collective-permute-done.5 = bf16[768,4096]{1,0:T(8,128)(2,1)} collective-permute-done((bf16[768,4096]{1,0:T(8,128)(2,1)S(1)}, bf16[768,4096]{1,0:T(8,128)(2,1)}, u32[]{:S(2)}, u32[]{:S(2)}) %collective-permute-start.5) | collective-permute-done | bytes 6291488 | tf_op jit(solution)/shard_map/ppermute | solution.py:17
  317.6 9.4 fusion.13
  327.0 274.8 %collective-permute-done.9 = bf16[768,4096]{1,0:T(8,128)(2,1)S(1)} collective-permute-done((bf16[768,4096]{1,0:T(8,128)(2,1)S(1)}, bf16[768,4096]{1,0:T(8,128)(2,1)S(1)}, u32[]{:S(2)}, u32[]{:S(2)}) %collective-permute-start.9) | collective-permute-done | bytes 6291488 | tf_op jit(solution)/shard_map/ppermute | solution.py:17
  601.8 6.6 fusion.14
  608.4 93.5 %collective-permute-done.1 = bf16[768,4096]{1,0:T(8,128)(2,1)S(1)} collective-permute-done((bf16[768,4096]{1,0:T(8,128)(2,1)S(1)}, bf16[768,4096]{1,0:T(8,128)(2,1)S(1)}, u32[]{:S(2)}, u32[]{:S(2)}) %collective-permute-start.1) | collective-permute-done | bytes 6291488 | tf_op jit(solution)/shard_map/ppermute | solution.py:17
  701.9 6.5 fusion.12
  708.4 0.0 copy-start.1
  708.4 0.0 copy-start.2
  708.4 0.0 all-reduce.3.cloned.1.call-update
  708.4 181.5 %all-reduce.3.cloned.1.call-done = (f32[768,768]{1,0:T(8,128)}, f32[768,768]{1,0:T(8,128)}, f32[768,768]{1,0:T(8,128)}) async-done(((f32[768,768]{1,0:T(8,128)}, f32[768,768]{1,0:T(8,128)}, f32[768,768]{1,0:T(8,128)}), (f32[768,768]{1,0:T(8,128)}, f32[768,768]{1,0:T(8,128)}, f32[768,768]{1,0:T(8,128)})) %all-reduce.3.cloned.1.call-update) | async-done | bytes 7077904 | tf_op jit(solution)/shard_map/psum | solution.py:52
  889.9 1.0 collective-permute-start.11
  890.8 2.4 collective-permute-start.3
  893.2 0.6 collective-permute-start.7
  893.8 0.0 copy-done.1
  893.8 0.0 copy-done.2
  893.8 6.6 collective-permute-start.8
  900.4 1.8 collective-permute-start.4
  902.2 18.2 %collective-permute-done.8 = s32[2,768]{1,0:T(2,128)S(1)} collective-permute-done((s32[2,768]{1,0:T(2,128)S(1)}, s32[2,768]{1,0:T(2,128)S(1)}, u32[]{:S(2)}, u32[]{:S(2)}) %collective-permute-start.8) | collective-permute-done | bytes 6176 | tf_op jit(solution)/shard_map/ppermute | solution.py:17
  920.4 0.0 collective-permute-start.10
  920.4 0.0 collective-permute-done.4
  920.4 0.1 collective-permute-start
  920.5 76.1 %collective-permute-done = s32[2,768]{1,0:T(2,128)S(1)} collective-permute-done((s32[2,768]{1,0:T(2,128)S(1)}, s32[2,768]{1,0:T(2,128)S(1)}, u32[]{:S(2)}, u32[]{:S(2)}) %collective-permute-start) | collective-permute-done | bytes 6176 | tf_op jit(solution)/shard_map/ppermute | solution.py:17
  996.7 2.4 collective-permute-start.2
  999.1 0.0 copy-start
  999.1 0.0 collective-permute-done.10
  999.1 155.2 %collective-permute-start.6 = (s32[768]{0:T(1024)S(1)}, s32[768]{0:T(1024)S(1)}, u32[]{:S(2)}, u32[]{:S(2)}) collective-permute-start(s32[768]{0:T(1024)S(1)} %copy-done.1), channel_id=1, source_target_pairs={{0,4},{2,6},{4,8},{6,10},{8,12},{10,14},{12,16},{14,18},{16,20},{1... | collective-permute-start | bytes 9224 | tf_op jit(solution)/shard_map/ppermute | solution.py:17
  1154.3 3.7 add_divide_fusion.1
  1157.9 0.0 collective-permute-done.2
  1158.0 0.0 collective-permute-done.6
  1158.0 0.0 collective-permute-done.11
  1158.0 0.0 collective-permute-done.3
  1158.0 0.0 collective-permute-done.7
  1158.0 0.0 copy-done
  1158.0 4.8 fusion.9
  1162.8 0.5 fusion.11
  1163.4 0.6 fusion.8
  (17 shorter events, 0.1 us)
Async XLA Ops:
  6.5 883.4 %all-reduce.3.cloned.1.call-start = ((), (), s32[]{:S(2)}) async-start(), calls=%async_computation | async-start | bytes 14155776 | tf_op jit(solution)/shard_map/psum | solution.py:52
  20.4 297.2 %collective-permute-start.5 = (bf16[768,4096]{1,0:T(8,128)(2,1)S(1)}, bf16[768,4096]{1,0:T(8,128)(2,1)}, u32[]{:S(2)}, u32[]{:S(2)}) collective-permute-start(bf16[768,4096]{1,0:T(8,128)(2,1)S(1)} %fusion.1), channel_id=1, source_target_pairs={{0,252},{2,254},{4,0},{6,2},{8,4},{10,6},{12,8},{14,10},{16,12},{1... | collective-permute-start | bytes 18874376 | tf_op jit(solution)/shard_map/ppermute | solution.py:17
  30.5 571.3 %collective-permute-start.9 = (bf16[768,4096]{1,0:T(8,128)(2,1)S(1)}, bf16[768,4096]{1,0:T(8,128)(2,1)S(1)}, u32[]{:S(2)}, u32[]{:S(2)}) collective-permute-start(bf16[768,4096]{1,0:T(8,128)(2,1)S(1)} %fusion.1), channel_id=1, source_target_pairs={{0,250},{2,252},{4,254},{6,0},{8,2},{10,4},{12,6},{14,8},{16,10},{... | collective-permute-start | bytes 18874376 | tf_op jit(solution)/shard_map/ppermute | solution.py:17
  30.5 671.4 %collective-permute-start.1 = (bf16[768,4096]{1,0:T(8,128)(2,1)S(1)}, bf16[768,4096]{1,0:T(8,128)(2,1)S(1)}, u32[]{:S(2)}, u32[]{:S(2)}) collective-permute-start(bf16[768,4096]{1,0:T(8,128)(2,1)S(1)} %fusion.1), channel_id=1, source_target_pairs={{0,254},{2,0},{4,2},{6,4},{8,6},{10,8},{12,10},{14,12},{16,14},{18... | collective-permute-start | bytes 18874376 | tf_op jit(solution)/shard_map/ppermute | solution.py:17
  708.4 185.4 %copy-start.1 = (s32[768]{0:T(1024)S(1)}, s32[768]{0:T(1024)}, u32[]{:S(2)}) copy-start(s32[768]{0:T(1024)} %param.4) | copy-start | bytes 9220
  708.4 185.4 %copy-start.2 = (s32[768]{0:T(1024)S(1)}, s32[768]{0:T(1024)}, u32[]{:S(2)}) copy-start(s32[768]{0:T(1024)} %param.5) | copy-start | bytes 9220
  889.9 268.1 %collective-permute-start.11 = (f32[768,768]{1,0:T(8,128)}, f32[768,768]{1,0:T(8,128)S(1)}, u32[]{:S(2)}, u32[]{:S(2)}) collective-permute-start(f32[768,768]{1,0:T(8,128)} %get-tuple-element.22), channel_id=1, source_target_pairs={{0,6},{2,8},{4,10},{6,12},{8,14},{10,16},{12,18},{14,20},{16,22},{... | collective-permute-start | bytes 7077896 | tf_op jit(solution)/shard_map/ppermute | solution.py:17
  890.8 267.1 %collective-permute-start.3 = (f32[768,768]{1,0:T(8,128)}, f32[768,768]{1,0:T(8,128)S(1)}, u32[]{:S(2)}, u32[]{:S(2)}) collective-permute-start(f32[768,768]{1,0:T(8,128)} %get-tuple-element.21), channel_id=1, source_target_pairs={{0,2},{2,4},{4,6},{6,8},{8,10},{10,12},{12,14},{14,16},{16,18},{18... | collective-permute-start | bytes 7077896 | tf_op jit(solution)/shard_map/ppermute | solution.py:17
  893.2 264.8 %collective-permute-start.7 = (f32[768,768]{1,0:T(8,128)}, f32[768,768]{1,0:T(8,128)S(1)}, u32[]{:S(2)}, u32[]{:S(2)}) collective-permute-start(f32[768,768]{1,0:T(8,128)} %get-tuple-element.23), channel_id=1, source_target_pairs={{0,4},{2,6},{4,8},{6,10},{8,12},{10,14},{12,16},{14,18},{16,20},{1... | collective-permute-start | bytes 7077896 | tf_op jit(solution)/shard_map/ppermute | solution.py:17
  893.8 26.6 %collective-permute-start.8 = (s32[2,768]{1,0:T(2,128)S(1)}, s32[2,768]{1,0:T(2,128)S(1)}, u32[]{:S(2)}, u32[]{:S(2)}) collective-permute-start(s32[2,768]{1,0:T(2,128)S(1)} %pad_add_fusion), channel_id=1, source_target_pairs={{0,250},{2,252},{4,254},{6,0},{8,2},{10,4},{12,6},{14,8},{16,10},{... | collective-permute-start | bytes 18440 | tf_op jit(solution)/shard_map/ppermute | solution.py:17
  900.4 20.0 %collective-permute-start.4 = (s32[2,768]{1,0:T(2,128)S(1)}, s32[2,768]{1,0:T(2,128)S(1)}, u32[]{:S(2)}, u32[]{:S(2)}) collective-permute-start(s32[2,768]{1,0:T(2,128)S(1)} %pad_add_fusion), channel_id=1, source_target_pairs={{0,252},{2,254},{4,0},{6,2},{8,4},{10,6},{12,8},{14,10},{16,12},{1... | collective-permute-start | bytes 18440 | tf_op jit(solution)/shard_map/ppermute | solution.py:17
  920.4 78.7 %collective-permute-start.10 = (s32[768]{0:T(1024)S(1)}, s32[768]{0:T(1024)S(1)}, u32[]{:S(2)}, u32[]{:S(2)}) collective-permute-start(s32[768]{0:T(1024)S(1)} %copy-done.1), channel_id=1, source_target_pairs={{0,6},{2,8},{4,10},{6,12},{8,14},{10,16},{12,18},{14,20},{16,22},{... | collective-permute-start | bytes 9224 | tf_op jit(solution)/shard_map/ppermute | solution.py:17
  920.4 76.2 %collective-permute-start = (s32[2,768]{1,0:T(2,128)S(1)}, s32[2,768]{1,0:T(2,128)S(1)}, u32[]{:S(2)}, u32[]{:S(2)}) collective-permute-start(s32[2,768]{1,0:T(2,128)S(1)} %pad_add_fusion), channel_id=1, source_target_pairs={{0,254},{2,0},{4,2},{6,4},{8,6},{10,8},{12,10},{14,12},{16,14},{18... | collective-permute-start | bytes 18440 | tf_op jit(solution)/shard_map/ppermute | solution.py:17
  996.7 161.3 %collective-permute-start.2 = (s32[768]{0:T(1024)S(1)}, s32[768]{0:T(1024)S(1)}, u32[]{:S(2)}, u32[]{:S(2)}) collective-permute-start(s32[768]{0:T(1024)S(1)} %copy-done.1), channel_id=1, source_target_pairs={{0,2},{2,4},{4,6},{6,8},{8,10},{10,12},{12,14},{14,16},{16,18},{18... | collective-permute-start | bytes 9224 | tf_op jit(solution)/shard_map/ppermute | solution.py:17
  999.1 158.9 %copy-start = (f32[768,768]{1,0:T(8,128)S(1)}, f32[768,768]{1,0:T(8,128)}, u32[]{:S(2)}) copy-start(f32[768,768]{1,0:T(8,128)} %get-tuple-element.21) | copy-start | bytes 7077892
  999.1 158.9 %collective-permute-start.6 = (s32[768]{0:T(1024)S(1)}, s32[768]{0:T(1024)S(1)}, u32[]{:S(2)}, u32[]{:S(2)}) collective-permute-start(s32[768]{0:T(1024)S(1)} %copy-done.1), channel_id=1, source_target_pairs={{0,4},{2,6},{4,8},{6,10},{8,12},{10,14},{12,16},{14,18},{16,20},{1... | collective-permute-start | bytes 9224 | tf_op jit(solution)/shard_map/ppermute | solution.py:17
Sparse Core Ops, SparseCore 0:
  708.5 181.3 all-reduce.2
where the time goes:
time: 1170 us
  waiting for transfers between devices  930 us (79%)
  starting transfers between devices  181 us (15%)
  matrix products  22.5 us (2%)
  other arithmetic  18.5 us (2%)
  between operations  13.6 us (1%)
    ppermute x12, waiting for transfers between devices, from_behind(): return lax.ppermute(value, axis, pairs)  749 us
    psum x1, waiting for transfers between devices, local(): score_matrix = lax.psum(partial_value, 'feat')  181 us
    ppermute x12, starting transfers between devices, from_behind(): return lax.ppermute(value, axis, pairs)  181 us
  transfers between devices with their start and end apart: 13, of which 6 were waited for; matrix products, arithmetic and copies ran while one was open for 2% of the time, Pallas kernels for 0%

commit v1 on v0

v1 whole, which is shorter than its diff:
```python
import functools
import math

import jax
import jax.numpy as jnp
from jax import lax
from jax.experimental import pallas as pl
from jax.experimental.pallas import tpu as pltpu
from jax.sharding import PartitionSpec as P

CHUNK = 128
SCALE = math.log2(math.e) / 0.02
MESH = pl.DeviceIdType.MESH
F32 = jnp.float32


def turn(row):
    return jnp.broadcast_to(row, (CHUNK, CHUNK)).T


def kernel(
    rows_count, full_width,
    x_hbm, group_ref, code_ref, out_ref,
    own, slot_a, slot_b, slot_c, unit,
    keep, sent, got,
    squares, squares_in, meta, meta_a, meta_b, meta_c,
    group_own, level_own, group_far, level_far,
    acc_own, acc_far,
    count_a, count_b, count_c, total, in_a, in_b, in_c, in_d, in_f,
    load_sem, fwd_send, a_recv, relay_send, b_recv, back_send, part_send, c_recv,
    job_send, job_recv, small_send, small_recv,
):
    rows, width = own.shape
    half = rows // 2
    steps = rows // CHUNK
    turnover = steps // 2
    me = lax.axis_index("rows")
    feat = lax.axis_index("feat")
    core = lax.rem(me, 2)
    other = me + 1 - 2 * core
    fwd = lax.rem(me + 2, rows_count)
    back = lax.rem(me + rows_count - 2, rows_count)
    fwd_other = lax.rem(other + 2, rows_count)
    back_other = lax.rem(other + rows_count - 2, rows_count)
    mate = (me, 1 - feat)
    first = core == 0
    second = core == 1

    def part(j):
        return pl.ds(pl.multiple_of(j * CHUNK, CHUNK), CHUNK)

    def remote(source, target, send, recv, where):
        return pltpu.make_async_remote_copy(
            src_ref=source, dst_ref=target, send_sem=send, recv_sem=recv,
            device_id=where, device_id_type=MESH,
        )

    def load(j):
        return pltpu.make_async_copy(x_hbm.at[part(j)], own.at[part(j)], load_sem.at[j])

    def fwd_copy(j):
        return remote(x_hbm.at[part(j)], slot_a.at[part(j)], fwd_send.at[j], a_recv.at[j], (fwd, feat))

    def relay_copy(j):
        return remote(slot_a.at[part(j)], slot_b.at[part(j)], relay_send.at[j], b_recv.at[j], (other, feat))

    def back_copy(j):
        return remote(x_hbm.at[part(j)], slot_c.at[part(j)], back_send.at[j], c_recv.at[j], (back, feat))

    def part_copy(j):
        return remote(x_hbm.at[part(j)], slot_c.at[part(j)], part_send.at[j], c_recv.at[j], (other, feat))

    def job_copy(t):
        return remote(sent.at[t], got.at[t], job_send.at[t], job_recv.at[t], mate)

    def small(n, source, target, where):
        return remote(source, target, small_send.at[n], small_recv.at[n], where)

    squares_copy = small(0, squares, squares_in, mate)
    meta_fwd = small(1, meta, meta_a, (fwd, feat))
    meta_fwd_other = small(2, meta, meta_b, (fwd_other, feat))
    meta_back = remote(meta, meta_c, small_send.at[3], small_recv.at[3], (back, feat))
    meta_part = remote(meta, meta_c, small_send.at[4], small_recv.at[3], (other, feat))
    a_home = small(5, count_a, in_a, (back, feat))
    b_home = small(6, count_b, in_b, (back_other, feat))
    c_home_fwd = small(7, count_c, in_c, (fwd, feat))
    c_home_part = small(8, count_c, in_d, (other, feat))
    final = small(9, total, in_f, mate)

    for j in range(steps):
        load(j).start()
    barrier = pltpu.get_barrier_semaphore()
    peers = [(fwd, feat), (fwd_other, feat), (back, feat), (back_other, feat), (other, feat), mate]
    for peer in peers:
        pl.semaphore_signal(barrier, inc=1, device_id=peer, device_id_type=MESH)
    pl.semaphore_wait(barrier, len(peers))

    for j in range(steps):
        fwd_copy(j).start()

    @pl.when(first)
    def _():
        for j in range(steps):
            part_copy(j).start()
        for j in range(steps):
            back_copy(j).start()

    def square(j, carry):
        load(j).wait()
        added = jnp.zeros((CHUNK, CHUNK), F32)
        for t in range(width // CHUNK):
            piece = own[part(j), t * CHUNK : (t + 1) * CHUNK].astype(F32)
            added = added + piece * piece
        squares[0:1, part(j)] = jnp.sum(added.T, axis=0, keepdims=True)
        return carry

    squares[...] = jnp.zeros_like(squares)
    lax.fori_loop(0, steps, square, 0)
    squares_copy.start()
    squares_copy.wait_recv()
    inverse = lax.rsqrt((squares[0:1, :] + squares_in[0:1, :]) / full_width + 1e-06) / math.sqrt(full_width)
    meta[...] = jnp.zeros_like(meta)
    meta[0:1, :] = inverse
    meta[1:2, :] = group_ref[...].astype(F32)
    meta[2:3, :] = jnp.exp2((0.2 + 0.15 * code_ref[...].astype(F32)) * SCALE)
    meta_fwd.start()
    meta_fwd_other.start()

    @pl.when(first)
    def _():
        meta_part.start()
        meta_back.start()

    def normalize(source, j, target, into, meta_ref):
        factor = turn(meta_ref[0:1, part(j)])
        for t in range(width // CHUNK):
            lanes = slice(t * CHUNK, (t + 1) * CHUNK)
            target[into, lanes] = (source[part(j), lanes].astype(F32) * factor).astype(jnp.bfloat16)

    def own_unit(j, carry):
        normalize(own, j, own, part(j), meta)
        return carry

    lax.fori_loop(0, steps, own_unit, 0)

    def columns(meta_ref, group_col, level_col):
        for i in range(half // CHUNK):
            lanes = part(feat * (half // CHUNK) + i)
            group_col[i * CHUNK : (i + 1) * CHUNK, :] = turn(meta_ref[1:2, lanes])
            level_col[i * CHUNK : (i + 1) * CHUNK, :] = turn(meta_ref[2:3, lanes])

    columns(meta, group_own, level_own)
    acc_own[...] = jnp.zeros_like(acc_own)
    acc_far[...] = jnp.zeros_like(acc_far)
    for ref in (count_a, count_b, count_c, total):
        ref[...] = jnp.zeros_like(ref)

    def job(t, fixed, moving, at):
        chunk = moving[at, :]
        for where, target in ((1 - feat, sent), (feat, keep)):
            lines = pl.ds(pl.multiple_of(where * half, half), half)
            target[t] = lax.dot_general(
                fixed[lines, :], chunk, (((1,), (1,)), ((), ())), preferred_element_type=F32
            )
            if target is sent:
                job_copy(t).start()

    size = 32

    def finish(t, j, group_col, level_col, acc, meta_ref, count):
        job_copy(t).wait_recv()
        group_row = jnp.broadcast_to(meta_ref[1:2, part(j)], (size, CHUNK))
        level_row = jnp.broadcast_to(meta_ref[2:3, part(j)], (size, CHUNK))

        def piece(i, carry):
            matched, overall = carry
            at = pl.ds(pl.multiple_of(i * size, size), size)
            power = jnp.exp2((keep[t, at, :] + got[t, at, :]) * (-SCALE))
            mine = 1.0 / (1.0 + level_col[at, :] * power)
            yours = 1.0 / (1.0 + level_row * power)
            same = group_col[at, :] == group_row
            acc[0, at, :] += jnp.where(same, mine, 0.0)
            acc[1, at, :] += mine
            return matched + jnp.where(same, yours, 0.0), overall + yours

        zero = jnp.zeros((size, CHUNK), F32)
        matched, overall = lax.fori_loop(0, half // size, piece, (zero, zero))
        count[0:1, part(j)] += jnp.sum(matched, axis=0, keepdims=True)
        count[1:2, part(j)] += jnp.sum(overall, axis=0, keepdims=True)

    def finish_a(j):
        finish(steps + j, j, group_own, level_own, acc_own, meta_a, count_a)

    def finish_b(j):
        finish(2 * steps + j, j, group_own, level_own, acc_own, meta_b, count_b)

    def finish_near(j):
        finish(j, j, group_own, level_own, acc_own, meta_c, count_c)

    def finish_far(j):
        finish(j, j, group_far, level_far, acc_far, meta_b, count_b)

    meta_wait_c = remote(meta, meta_c, small_send.at[3], small_recv.at[3], (back, feat))

    @pl.when(second)
    def _():
        meta_wait_c.wait_recv()

        def step(j, carry):
            part_copy(j).wait_recv()
            normalize(slot_c, j, slot_c, part(j), meta_c)
            job(j, own, slot_c, part(j))
            return carry

        lax.fori_loop(0, steps, step, 0)

    meta_fwd.wait_recv()
    meta_fwd_other.wait_recv()

    def main(j, carry):
        @pl.when(j > 0)
        def _():
            finish_a(j - 1)
            finish_b(j - 1)

        @pl.when(second)
        def _():
            finish_near(j)

        @pl.when(jnp.logical_and(first, j > turnover))
        def _():
            def old(i, carry):
                finish_far(i)
                return carry

            lax.fori_loop(jnp.where(j == turnover + 1, 0, j - 1), j, old, 0)

        fwd_copy(j).wait_recv()
        relay_copy(j).start()
        normalize(slot_a, j, unit, slice(0, CHUNK), meta_a)
        job(steps + j, own, unit, slice(0, CHUNK))
        relay_copy(j).wait_recv()
        normalize(slot_b, j, slot_b, part(j), meta_b)
        job(2 * steps + j, own, slot_b, part(j))

        @pl.when(jnp.logical_and(first, j == turnover))
        def _():
            meta_wait_c.wait_recv()

            def ready(i, carry):
                back_copy(i).wait_recv()
                normalize(slot_c, i, slot_c, part(i), meta_c)
                return carry

            lax.fori_loop(0, steps, ready, 0)
            columns(meta_c, group_far, level_far)

        @pl.when(jnp.logical_and(first, j >= turnover))
        def _():
            def far(i, carry):
                job(i, slot_c, slot_b, part(i))
                return carry

            lax.fori_loop(jnp.where(j == turnover, 0, j), j + 1, far, 0)

        return carry

    lax.fori_loop(0, steps, main, 0)
    finish_a(steps - 1)
    a_home.start()
    finish_b(steps - 1)

    def fold(acc, count, add):
        for i in range(half // CHUNK):
            lanes = part(feat * (half // CHUNK) + i)
            for n in range(2):
                value = jnp.sum(acc[n, i * CHUNK : (i + 1) * CHUNK, :].T, axis=0, keepdims=True)
                count[n : n + 1, lanes] = value

    @pl.when(first)
    def _():
        finish_far(steps - 1)
        fold(acc_far, count_c, False)

    b_home.start()

    @pl.when(first)
    def _():
        c_home_fwd.start()

    @pl.when(second)
    def _():
        c_home_part.start()

    fold(acc_own, total, False)
    a_home.wait_recv()
    b_home.wait_recv()
    total[...] += in_a[...] + in_b[...]

    @pl.when(first)
    def _():
        c_home_fwd.wait_recv()
        c_home_part.wait_recv()
        total[...] += in_c[...] + in_d[...]

    final.start()
    final.wait_recv()
    matched = total[0:1, :] + in_f[0:1, :]
    overall = total[1:2, :] + in_f[1:2, :]
    out_ref[0:1, :] = matched
    out_ref[1:2, :] = overall - matched

    def drain(j, carry):
        fwd_copy(j).wait_send()
        relay_copy(j).wait_send()
        return carry

    lax.fori_loop(0, steps, drain, 0)

    def drain_jobs(t, carry):
        job_copy(t).wait_send()
        return carry

    lax.fori_loop(0, 3 * steps, drain_jobs, 0)
    for copy in (squares_copy, meta_fwd, meta_fwd_other, a_home, b_home, final):
        copy.wait_send()

    @pl.when(first)
    def _():
        def drain_c(j, carry):
            part_copy(j).wait_send()
            back_copy(j).wait_send()
            return carry

        lax.fori_loop(0, steps, drain_c, 0)
        meta_part.wait_send()
        meta_back.wait_send()
        c_home_fwd.wait_send()

    @pl.when(second)
    def _():
        c_home_part.wait_send()


def local(rows_count, features, group_index_list, threshold_codes):
    rows, width = features.shape
    full_width = width * lax.axis_size("feat")
    half = rows // 2
    steps = rows // CHUNK
    block = pltpu.VMEM((rows, width), jnp.bfloat16)
    tiles = pltpu.VMEM((3 * steps, half, CHUNK), F32)
    line = pltpu.VMEM((8, rows), F32)
    column = pltpu.VMEM((half, CHUNK), F32)
    sums = pltpu.VMEM((2, half, CHUNK), F32)
    sems = pltpu.SemaphoreType.DMA((steps,))
    vmem = pl.BlockSpec(memory_space=pltpu.VMEM)
    return pl.pallas_call(
        functools.partial(kernel, rows_count, full_width),
        out_shape=jax.ShapeDtypeStruct((2, rows), F32),
        in_specs=[pl.BlockSpec(memory_space=pl.ANY), vmem, vmem],
        out_specs=vmem,
        scratch_shapes=[
            block, block, block, block, pltpu.VMEM((CHUNK, width), jnp.bfloat16),
            tiles, tiles, tiles,
            *[line] * 6,
            *[column] * 4,
            sums, sums,
            *[line] * 9,
            *[sems] * 8,
            pltpu.SemaphoreType.DMA((3 * steps,)), pltpu.SemaphoreType.DMA((3 * steps,)),
            pltpu.SemaphoreType.DMA((10,)), pltpu.SemaphoreType.DMA((10,)),
        ],
        compiler_params=pltpu.CompilerParams(
            collective_id=0, has_side_effects=True, vmem_limit_bytes=56 * 1024 * 1024
        ),
    )(features, group_index_list.reshape(1, rows), threshold_codes.reshape(1, rows))


def solution(mesh):
    placed = (P("rows", "feat"), P("rows"), P("rows"))
    return jax.shard_map(
        functools.partial(local, mesh.shape["rows"]),
        mesh=mesh, in_specs=placed, out_specs=P(None, "rows"), check_vma=False,
    )
```

time: 1170 us -> 410 us (0.35)
  waiting for transfers between devices: 930 us -> 0 us
  Pallas kernels: 0 us -> 405 us
  starting transfers between devices: 181 us -> 0 us
  matrix products: 22.5 us -> 0 us
  other arithmetic: 18.5 us -> 0 us
  between operations: 13.6 us -> 0.01 us
    ppermute x12 -> x0, waiting for transfers between devices: 749 us -> none  [from_behind(): return lax.ppermute(value, axis, pairs)]
    pallas_call x0 -> x1, Pallas kernels: none -> 405 us  [local(): pl.pallas_call(functools.partial(kernel, rows_count, full_width), out_sha...]
    psum x1 -> x0, waiting for transfers between devices: 181 us -> none  [local(): score_matrix = lax.psum(partial_value, 'feat')]
    ppermute x12 -> x0, starting transfers between devices: 181 us -> none  [from_behind(): return lax.ppermute(value, axis, pairs)]
    dot_general x3 -> x0, matrix products: 22.5 us -> none  [local(): lax.dot_general(normed, partner, (((1,), (1,)), ((), ())), preferred_elem...]
  transfers between devices with their start and end apart: 13 -> 0, of which waited for: 6 -> 0; matrix products, arithmetic and copies ran while one was open for 2% -> 0% of each run, Pallas kernels for 0% -> 0%
where the time goes in v1:
time: 410 us; the launch traced here: 409 us
  Pallas kernels  405 us (99%)
    pallas_call x1, Pallas kernels, local(): pl.pallas_call(functools.partial(kernel, rows_count, full_width), out_sha...  405 us

profile of v1, /device:TPU:32, one launch (start us, length us, event | category | flops | bytes accessed | tf_op | source)
XLA Modules:
  0.0 408.9 jit_solution(4020091349249035836)
XLA Ops:
  0.0 1.3 reshape.6.group_ref
  1.3 1.3 reshape.7.code_ref
  2.5 405.1 %shard_map.37 = f32[2,768]{1,0:T(2,128)} custom-call(bf16[768,4096]{1,0:T(8,128)(2,1)} %x_hbm.1, s32[1,768]{1,0:T(1,128)} %reshape.6.group_ref, s32[1,768]{1,0:T(1,128)} %reshape.7.code_ref), custom_call_target="tpu_custom_call" | custom-call | tf_op jit(solution)/shard_map/pallas_call | solution.py:357
  407.6 1.3 copy.5

commit v2 on v1

--- a/solution.py
+++ b/solution.py
@@ -11,6 +11,8 @@
 CHUNK = 128
 SCALE = math.log2(math.e) / 0.02
 MESH = pl.DeviceIdType.MESH
+PLANE = 16
+GRID = 32000.0
 F32 = jnp.float32
 
 
@@ -21,19 +23,19 @@
 def kernel(
     rows_count, full_width,
     x_hbm, group_ref, code_ref, out_ref,
-    own, slot_a, slot_b, slot_c, unit,
+    own, slot_a, slot_b, slot_c, hop, unit,
     keep, sent, got,
     squares, squares_in, meta, meta_a, meta_b, meta_c,
     group_own, level_own, group_far, level_far,
     acc_own, acc_far,
     count_a, count_b, count_c, total, in_a, in_b, in_c, in_d, in_f,
     load_sem, fwd_send, a_recv, relay_send, b_recv, back_send, part_send, c_recv,
-    job_send, job_recv, small_send, small_recv,
+    job_send, job_recv, small_send, small_recv, hop_send, hop_recv,
 ):
     rows, width = own.shape
     half = rows // 2
     steps = rows // CHUNK
-    turnover = steps // 2
+    turnover = steps - 2
     me = lax.axis_index("rows")
     feat = lax.axis_index("feat")
     core = lax.rem(me, 2)
@@ -45,6 +47,12 @@
     mate = (me, 1 - feat)
     first = core == 0
     second = core == 1
+    place = lax.rem(me // 2, PLANE)
+    low, next_low, side, next_high, high = (place == n for n in (0, 1, PLANE - 4, PLANE - 2, PLANE - 1))
+    bound = 2 * PLANE
+
+    def shift(n):
+        return (lax.rem(me + n + rows_count, rows_count), feat)
 
     def part(j):
         return pl.ds(pl.multiple_of(j * CHUNK, CHUNK), CHUNK)
@@ -54,6 +62,54 @@
             src_ref=source, dst_ref=target, send_sem=send, recv_sem=recv,
             device_id=where, device_id_type=MESH,
         )
+
+    by_side = {1: 0, 4: 1}
+    by_row = {2: 0, 5: 1}
+    straight = (0, 3)
+
+    def leg_copy(j):
+        slot = by_side[j] if j in by_side else by_row[j]
+        return remote(
+            x_hbm.at[part(j)], hop.at[slot], fwd_send.at[j], hop_recv.at[slot], shift(-6 if j in by_side else -2)
+        )
+
+    def side_copy(j):
+        return remote(hop.at[by_side[j]], slot_a.at[part(j)], hop_send.at[by_side[j]], a_recv.at[j], shift(8))
+
+    def row_copy(j):
+        slot = by_row[j]
+        return remote(hop.at[slot], hop.at[slot], hop_send.at[slot], hop_recv.at[slot], shift(6))
+
+    def last_copy(j):
+        return remote(hop.at[by_row[j]], slot_a.at[part(j)], hop_send.at[by_row[j]], a_recv.at[j], shift(-2))
+
+    def back_leg_copy(j):
+        return remote(x_hbm.at[part(j)], hop.at[j], back_send.at[j], hop_recv.at[j], shift(bound - 2))
+
+    def high_copy(j):
+        return remote(hop.at[j], slot_c.at[part(j)], hop_send.at[j], c_recv.at[j], shift(-bound))
+
+    def send_fwd(js):
+        @pl.when(jnp.logical_not(high))
+        def _():
+            for j in js:
+                fwd_copy(j).start()
+
+    def send_back(js):
+        @pl.when(jnp.logical_and(first, low))
+        def _():
+            for j in js:
+                (back_leg_copy(j) if j < steps // 2 else back_copy(j)).start()
+
+        @pl.when(jnp.logical_and(first, jnp.logical_not(low)))
+        def _():
+            for j in js:
+                back_copy(j).start()
+
+    def pass_on(*legs):
+        for arrived, copy in legs:
+            arrived.wait_recv()
+            copy.start()
 
     def load(j):
         return pltpu.make_async_copy(x_hbm.at[part(j)], own.at[part(j)], load_sem.at[j])
@@ -93,17 +149,33 @@
     peers = [(fwd, feat), (fwd_other, feat), (back, feat), (back_other, feat), (other, feat), mate]
     for peer in peers:
         pl.semaphore_signal(barrier, inc=1, device_id=peer, device_id_type=MESH)
-    pl.semaphore_wait(barrier, len(peers))
-
-    for j in range(steps):
-        fwd_copy(j).start()
+    expected = len(peers)
+    for role, offsets in (
+        (low, (bound - 2, -8)), (side, (6, 8)), (high, (2 - bound, -6, bound, -bound)),
+        (next_high, (6,)), (next_low, (-6,)),
+    ):
+        @pl.when(role)
+        def _():
+            for offset in offsets:
+                pl.semaphore_signal(barrier, inc=1, device_id=shift(offset), device_id_type=MESH)
+
+        expected += len(offsets) * role.astype(jnp.int32)
+    pl.semaphore_wait(barrier, expected)
+
+    @pl.when(high)
+    def _():
+        for j in by_row:
+            leg_copy(j).start()
+        fwd_copy(straight[0]).start()
+        leg_copy(1).start()
+
+    send_fwd((0,))
+    send_back((0,))
 
     @pl.when(first)
     def _():
         for j in range(steps):
             part_copy(j).start()
-        for j in range(steps):
-            back_copy(j).start()
 
     def square(j, carry):
         load(j).wait()
@@ -131,6 +203,13 @@
         meta_part.start()
         meta_back.start()
 
+    @pl.when(high)
+    def _():
+        leg_copy(4).start()
+
+    send_fwd((1, 2, 3, 4, 5))
+    send_back((1, 2, 3, 4, 5))
+
     def normalize(source, j, target, into, meta_ref):
         factor = turn(meta_ref[0:1, part(j)])
         for t in range(width // CHUNK):
@@ -159,9 +238,12 @@
         chunk = moving[at, :]
         for where, target in ((1 - feat, sent), (feat, keep)):
             lines = pl.ds(pl.multiple_of(where * half, half), half)
-            target[t] = lax.dot_general(
+            value = lax.dot_general(
                 fixed[lines, :], chunk, (((1,), (1,)), ((), ())), preferred_element_type=F32
             )
+            if target is sent:
+                value = jnp.round(value * GRID).astype(jnp.int32).astype(jnp.int16)
+            target[t] = value
             if target is sent:
                 job_copy(t).start()
 
@@ -175,7 +257,7 @@
         def piece(i, carry):
             matched, overall = carry
             at = pl.ds(pl.multiple_of(i * size, size), size)
-            power = jnp.exp2((keep[t, at, :] + got[t, at, :]) * (-SCALE))
+            power = jnp.exp2(keep[t, at, :] * (-SCALE) + got[t, at, :].astype(F32) * (-SCALE / GRID))
             mine = 1.0 / (1.0 + level_col[at, :] * power)
             yours = 1.0 / (1.0 + level_row * power)
             same = group_col[at, :] == group_row
@@ -218,10 +300,23 @@
     meta_fwd_other.wait_recv()
 
     def main(j, carry):
-        @pl.when(j > 0)
-        def _():
-            finish_a(j - 1)
-            finish_b(j - 1)
+        for turn_at, role, act in (
+            (1, high, lambda: fwd_copy(straight[1]).start()),
+            (1, side, lambda: pass_on((leg_copy(1), side_copy(1)))),
+            (3, side, lambda: pass_on((leg_copy(4), side_copy(4)))),
+            (1, next_high, lambda: pass_on((leg_copy(2), row_copy(2)))),
+            (3, next_high, lambda: pass_on((leg_copy(5), row_copy(5)))),
+            (3, next_low, lambda: pass_on((row_copy(2), last_copy(2)))),
+            (5, next_low, lambda: pass_on((row_copy(5), last_copy(5)))),
+            (1, jnp.logical_and(first, high), lambda: pass_on(*((back_leg_copy(i), high_copy(i)) for i in (0, 1)))),
+            (2, jnp.logical_and(first, high), lambda: pass_on((back_leg_copy(2), high_copy(2)))),
+        ):
+            pl.when(jnp.logical_and(j == turn_at, role))(act)
+
+        @pl.when(j > 1)
+        def _():
+            finish_a(j - 2)
+            finish_b(j - 2)
 
         @pl.when(second)
         def _():
@@ -266,6 +361,8 @@
         return carry
 
     lax.fori_loop(0, steps, main, 0)
+    finish_a(steps - 2)
+    finish_b(steps - 2)
     finish_a(steps - 1)
     a_home.start()
     finish_b(steps - 1)
@@ -316,6 +413,16 @@
         return carry
 
     lax.fori_loop(0, steps, drain, 0)
+    for role, copies in (
+        (side, (side_copy(1), side_copy(4))), (next_high, (row_copy(2), row_copy(5))),
+        (next_low, (last_copy(2), last_copy(5))),
+        (jnp.logical_and(first, high), (high_copy(0), high_copy(1), high_copy(2))),
+    ):
+        @pl.when(role)
+        def _():
+            for copy in copies:
+                copy.wait_send()
+
 
     def drain_jobs(t, carry):
         job_copy(t).wait_send()
@@ -349,6 +456,8 @@
     steps = rows // CHUNK
     block = pltpu.VMEM((rows, width), jnp.bfloat16)
     tiles = pltpu.VMEM((3 * steps, half, CHUNK), F32)
+    coded = pltpu.VMEM((3 * steps, half, CHUNK), jnp.int16)
+    hops = steps // 2
     line = pltpu.VMEM((8, rows), F32)
     column = pltpu.VMEM((half, CHUNK), F32)
     sums = pltpu.VMEM((2, half, CHUNK), F32)
@@ -360,8 +469,9 @@
         in_specs=[pl.BlockSpec(memory_space=pl.ANY), vmem, vmem],
         out_specs=vmem,
         scratch_shapes=[
-            block, block, block, block, pltpu.VMEM((CHUNK, width), jnp.bfloat16),
-            tiles, tiles, tiles,
+            block, block, block, block, pltpu.VMEM((hops, CHUNK, width), jnp.bfloat16),
+            pltpu.VMEM((CHUNK, width), jnp.bfloat16),
+            tiles, coded, coded,
             *[line] * 6,
             *[column] * 4,
             sums, sums,
@@ -369,6 +479,7 @@
             *[sems] * 8,
             pltpu.SemaphoreType.DMA((3 * steps,)), pltpu.SemaphoreType.DMA((3 * steps,)),
             pltpu.SemaphoreType.DMA((10,)), pltpu.SemaphoreType.DMA((10,)),
+            pltpu.SemaphoreType.DMA((hops,)), pltpu.SemaphoreType.DMA((hops,)),
         ],
         compiler_params=pltpu.CompilerParams(
             collective_id=0, has_side_effects=True, vmem_limit_bytes=56 * 1024 * 1024

time: 410 us -> 213 us (0.52)
  Pallas kernels: 405 us -> 208 us
    pallas_call x1, Pallas kernels: 405 us -> 208 us  [local(): pl.pallas_call(functools.partial(kernel, rows_count, full_width), out_sha...]
where the time goes in v2:
time: 213 us; the launch traced here: 212 us
  Pallas kernels  208 us (98%)
  local copies, waits for them, and re-layouts  3.83 us (2%)
    pallas_call x1, Pallas kernels, local(): pl.pallas_call(functools.partial(kernel, rows_count, full_width), out_sha...  208 us

profile of v2, /device:TPU:32, one launch (start us, length us, event | category | flops | bytes accessed | tf_op | source)
XLA Modules:
  0.0 211.7 jit_solution(7967819201324566841)
XLA Ops:
  0.0 1.3 reshape.6.group_ref
  1.3 1.3 reshape.7.code_ref
  2.5 207.8 %shard_map.37 = f32[2,768]{1,0:T(2,128)} custom-call(bf16[768,4096]{1,0:T(8,128)(2,1)} %x_hbm.1, s32[1,768]{1,0:T(1,128)} %reshape.6.group_ref, s32[1,768]{1,0:T(1,128)} %reshape.7.code_ref), custom_call_target="tpu_custom_call" | custom-call | tf_op jit(solution)/shard_map/pallas_call | solution.py:466
  210.4 1.3 copy.5

commit v3 on v2

--- a/solution.py
+++ b/solution.py
@@ -24,13 +24,13 @@
     rows_count, full_width,
     x_hbm, group_ref, code_ref, out_ref,
     own, slot_a, slot_b, slot_c, hop, unit,
-    keep, sent, got,
+    keep, sent, got, keep_pair, sent_pair, got_pair,
     squares, squares_in, meta, meta_a, meta_b, meta_c,
     group_own, level_own, group_far, level_far,
     acc_own, acc_far,
     count_a, count_b, count_c, total, in_a, in_b, in_c, in_d, in_f,
     load_sem, fwd_send, a_recv, relay_send, b_recv, back_send, part_send, c_recv,
-    job_send, job_recv, small_send, small_recv, hop_send, hop_recv,
+    job_send, job_recv, pair_send, pair_recv, small_send, small_recv, hop_send, hop_recv,
 ):
     rows, width = own.shape
     half = rows // 2
@@ -129,6 +129,9 @@
     def job_copy(t):
         return remote(sent.at[t], got.at[t], job_send.at[t], job_recv.at[t], mate)
 
+    def pair_copy(t):
+        return remote(sent_pair.at[t], got_pair.at[t], pair_send.at[t], pair_recv.at[t], mate)
+
     def small(n, source, target, where):
         return remote(source, target, small_send.at[n], small_recv.at[n], where)
 
@@ -166,7 +169,6 @@
     def _():
         for j in by_row:
             leg_copy(j).start()
-        fwd_copy(straight[0]).start()
         leg_copy(1).start()
 
     send_fwd((0,))
@@ -206,15 +208,19 @@
     @pl.when(high)
     def _():
         leg_copy(4).start()
+        fwd_copy(straight[0]).start()
 
     send_fwd((1, 2, 3, 4, 5))
     send_back((1, 2, 3, 4, 5))
 
-    def normalize(source, j, target, into, meta_ref):
+    def normalize(source, j, target, into, meta_ref, also=None):
         factor = turn(meta_ref[0:1, part(j)])
         for t in range(width // CHUNK):
             lanes = slice(t * CHUNK, (t + 1) * CHUNK)
-            target[into, lanes] = (source[part(j), lanes].astype(F32) * factor).astype(jnp.bfloat16)
+            value = (source[part(j), lanes].astype(F32) * factor).astype(jnp.bfloat16)
+            target[into, lanes] = value
+            if also is not None:
+                also[CHUNK:, lanes] = value
 
     def own_unit(j, carry):
         normalize(own, j, own, part(j), meta)
@@ -234,30 +240,31 @@
     for ref in (count_a, count_b, count_c, total):
         ref[...] = jnp.zeros_like(ref)
 
-    def job(t, fixed, moving, at):
-        chunk = moving[at, :]
-        for where, target in ((1 - feat, sent), (feat, keep)):
+    def job(fixed, chunk, t, held, outgoing, copy):
+        for where, target in ((1 - feat, outgoing), (feat, held)):
             lines = pl.ds(pl.multiple_of(where * half, half), half)
             value = lax.dot_general(
                 fixed[lines, :], chunk, (((1,), (1,)), ((), ())), preferred_element_type=F32
             )
-            if target is sent:
-                value = jnp.round(value * GRID).astype(jnp.int32).astype(jnp.int16)
-            target[t] = value
-            if target is sent:
-                job_copy(t).start()
+            if target is outgoing:
+                target[t] = jnp.round(value * GRID).astype(jnp.int32).astype(jnp.int16)
+                copy(t).start()
+            else:
+                target[t] = value
+
+    def single(t, fixed, moving, at):
+        job(fixed, moving[at, :], t, keep, sent, job_copy)
 
     size = 32
 
-    def finish(t, j, group_col, level_col, acc, meta_ref, count):
-        job_copy(t).wait_recv()
+    def finish(held, arrived, t, lanes, j, group_col, level_col, acc, meta_ref, count):
         group_row = jnp.broadcast_to(meta_ref[1:2, part(j)], (size, CHUNK))
         level_row = jnp.broadcast_to(meta_ref[2:3, part(j)], (size, CHUNK))
 
         def piece(i, carry):
             matched, overall = carry
             at = pl.ds(pl.multiple_of(i * size, size), size)
-            power = jnp.exp2(keep[t, at, :] * (-SCALE) + got[t, at, :].astype(F32) * (-SCALE / GRID))
+            power = jnp.exp2(held[t, at, lanes] * (-SCALE) + arrived[t, at, lanes].astype(F32) * (-SCALE / GRID))
             mine = 1.0 / (1.0 + level_col[at, :] * power)
             yours = 1.0 / (1.0 + level_row * power)
             same = group_col[at, :] == group_row
@@ -270,17 +277,22 @@
         count[0:1, part(j)] += jnp.sum(matched, axis=0, keepdims=True)
         count[1:2, part(j)] += jnp.sum(overall, axis=0, keepdims=True)
 
+    every, left, right = slice(0, CHUNK), slice(0, CHUNK), slice(CHUNK, 2 * CHUNK)
+
     def finish_a(j):
-        finish(steps + j, j, group_own, level_own, acc_own, meta_a, count_a)
+        pair_copy(j).wait_recv()
+        finish(keep_pair, got_pair, j, left, j, group_own, level_own, acc_own, meta_a, count_a)
 
     def finish_b(j):
-        finish(2 * steps + j, j, group_own, level_own, acc_own, meta_b, count_b)
+        finish(keep_pair, got_pair, j, right, j, group_own, level_own, acc_own, meta_b, count_b)
 
     def finish_near(j):
-        finish(j, j, group_own, level_own, acc_own, meta_c, count_c)
+        job_copy(j).wait_recv()
+        finish(keep, got, j, every, j, group_own, level_own, acc_own, meta_c, count_c)
 
     def finish_far(j):
-        finish(j, j, group_far, level_far, acc_far, meta_b, count_b)
+        job_copy(j).wait_recv()
+        finish(keep, got, j, every, j, group_far, level_far, acc_far, meta_b, count_b)
 
     meta_wait_c = remote(meta, meta_c, small_send.at[3], small_recv.at[3], (back, feat))
 
@@ -291,7 +303,7 @@
         def step(j, carry):
             part_copy(j).wait_recv()
             normalize(slot_c, j, slot_c, part(j), meta_c)
-            job(j, own, slot_c, part(j))
+            single(j, own, slot_c, part(j))
             return carry
 
         lax.fori_loop(0, steps, step, 0)
@@ -302,10 +314,10 @@
     def main(j, carry):
         for turn_at, role, act in (
             (1, high, lambda: fwd_copy(straight[1]).start()),
-            (1, side, lambda: pass_on((leg_copy(1), side_copy(1)))),
-            (3, side, lambda: pass_on((leg_copy(4), side_copy(4)))),
-            (1, next_high, lambda: pass_on((leg_copy(2), row_copy(2)))),
-            (3, next_high, lambda: pass_on((leg_copy(5), row_copy(5)))),
+            (0, side, lambda: pass_on((leg_copy(1), side_copy(1)))),
+            (2, side, lambda: pass_on((leg_copy(4), side_copy(4)))),
+            (0, next_high, lambda: pass_on((leg_copy(2), row_copy(2)))),
+            (2, next_high, lambda: pass_on((leg_copy(5), row_copy(5)))),
             (3, next_low, lambda: pass_on((row_copy(2), last_copy(2)))),
             (5, next_low, lambda: pass_on((row_copy(5), last_copy(5)))),
             (1, jnp.logical_and(first, high), lambda: pass_on(*((back_leg_copy(i), high_copy(i)) for i in (0, 1)))),
@@ -318,6 +330,11 @@
             finish_a(j - 2)
             finish_b(j - 2)
 
+        @pl.when(j == steps - 1)
+        def _():
+            finish_a(j - 1)
+            finish_b(j - 1)
+
         @pl.when(second)
         def _():
             finish_near(j)
@@ -333,10 +350,9 @@
         fwd_copy(j).wait_recv()
         relay_copy(j).start()
         normalize(slot_a, j, unit, slice(0, CHUNK), meta_a)
-        job(steps + j, own, unit, slice(0, CHUNK))
         relay_copy(j).wait_recv()
-        normalize(slot_b, j, slot_b, part(j), meta_b)
-        job(2 * steps + j, own, slot_b, part(j))
+        normalize(slot_b, j, slot_b, part(j), meta_b, unit)
+        job(own, unit[...], j, keep_pair, sent_pair, pair_copy)
 
         @pl.when(jnp.logical_and(first, j == turnover))
         def _():
@@ -353,7 +369,7 @@
         @pl.when(jnp.logical_and(first, j >= turnover))
         def _():
             def far(i, carry):
-                job(i, slot_c, slot_b, part(i))
+                single(i, slot_c, slot_b, part(i))
                 return carry
 
             lax.fori_loop(jnp.where(j == turnover, 0, j), j + 1, far, 0)
@@ -361,8 +377,6 @@
         return carry
 
     lax.fori_loop(0, steps, main, 0)
-    finish_a(steps - 2)
-    finish_b(steps - 2)
     finish_a(steps - 1)
     a_home.start()
     finish_b(steps - 1)
@@ -426,9 +440,10 @@
 
     def drain_jobs(t, carry):
         job_copy(t).wait_send()
+        pair_copy(t).wait_send()
         return carry
 
-    lax.fori_loop(0, 3 * steps, drain_jobs, 0)
+    lax.fori_loop(0, steps, drain_jobs, 0)
     for copy in (squares_copy, meta_fwd, meta_fwd_other, a_home, b_home, final):
         copy.wait_send()
 
@@ -455,8 +470,9 @@
     half = rows // 2
     steps = rows // CHUNK
     block = pltpu.VMEM((rows, width), jnp.bfloat16)
-    tiles = pltpu.VMEM((3 * steps, half, CHUNK), F32)
-    coded = pltpu.VMEM((3 * steps, half, CHUNK), jnp.int16)
+    def tiles(wide, dtype):
+        return pltpu.VMEM((steps, half, wide), dtype)
+
     hops = steps // 2
     line = pltpu.VMEM((8, rows), F32)
     column = pltpu.VMEM((half, CHUNK), F32)
@@ -470,14 +486,13 @@
         out_specs=vmem,
         scratch_shapes=[
             block, block, block, block, pltpu.VMEM((hops, CHUNK, width), jnp.bfloat16),
-            pltpu.VMEM((CHUNK, width), jnp.bfloat16),
-            tiles, coded, coded,
+            pltpu.VMEM((2 * CHUNK, width), jnp.bfloat16),
+            *[tiles(w, t) for w in (CHUNK, 2 * CHUNK) for t in (F32, jnp.int16, jnp.int16)],
             *[line] * 6,
             *[column] * 4,
             sums, sums,
             *[line] * 9,
-            *[sems] * 8,
-            pltpu.SemaphoreType.DMA((3 * steps,)), pltpu.SemaphoreType.DMA((3 * steps,)),
+            *[sems] * 12,
             pltpu.SemaphoreType.DMA((10,)), pltpu.SemaphoreType.DMA((10,)),
             pltpu.SemaphoreType.DMA((hops,)), pltpu.SemaphoreType.DMA((hops,)),
         ],

time: 213 us -> 201 us (0.944); the launches traced: 212 us -> 198 us
  Pallas kernels: 208 us -> 194 us
    pallas_call x1, Pallas kernels: 208 us -> 194 us  [local(): pl.pallas_call(functools.partial(kernel, rows_count, full_width), out_sha...]
where the time goes in v3:
time: 201 us; the launch traced here: 198 us
  Pallas kernels  194 us (97%)
  local copies, waits for them, and re-layouts  3.83 us (2%)
    pallas_call x1, Pallas kernels, local(): pl.pallas_call(functools.partial(kernel, rows_count, full_width), out_sha...  194 us

profile of v3, /device:TPU:32, one launch (start us, length us, event | category | flops | bytes accessed | tf_op | source)
XLA Modules:
  0.0 197.5 jit_solution(17656923226844122560)
XLA Ops:
  0.0 1.3 reshape.6.group_ref
  1.3 1.3 reshape.7.code_ref
  2.5 193.7 %shard_map.37 = f32[2,768]{1,0:T(2,128)} custom-call(bf16[768,4096]{1,0:T(8,128)(2,1)} %x_hbm.1, s32[1,768]{1,0:T(1,128)} %reshape.6.group_ref, s32[1,768]{1,0:T(1,128)} %reshape.7.code_ref), custom_call_target="tpu_custom_call" | custom-call | tf_op jit(solution)/shard_map/pallas_call | solution.py:482
  196.2 1.3 copy.5

commit v4 on v3

--- a/solution.py
+++ b/solution.py
@@ -325,28 +325,6 @@
         ):
             pl.when(jnp.logical_and(j == turn_at, role))(act)
 
-        @pl.when(j > 1)
-        def _():
-            finish_a(j - 2)
-            finish_b(j - 2)
-
-        @pl.when(j == steps - 1)
-        def _():
-            finish_a(j - 1)
-            finish_b(j - 1)
-
-        @pl.when(second)
-        def _():
-            finish_near(j)
-
-        @pl.when(jnp.logical_and(first, j > turnover))
-        def _():
-            def old(i, carry):
-                finish_far(i)
-                return carry
-
-            lax.fori_loop(jnp.where(j == turnover + 1, 0, j - 1), j, old, 0)
-
         fwd_copy(j).wait_recv()
         relay_copy(j).start()
         normalize(slot_a, j, unit, slice(0, CHUNK), meta_a)
@@ -373,6 +351,28 @@
                 return carry
 
             lax.fori_loop(jnp.where(j == turnover, 0, j), j + 1, far, 0)
+
+        @pl.when(j > 1)
+        def _():
+            finish_a(j - 2)
+            finish_b(j - 2)
+
+        @pl.when(j == steps - 1)
+        def _():
+            finish_a(j - 1)
+            finish_b(j - 1)
+
+        @pl.when(second)
+        def _():
+            finish_near(j)
+
+        @pl.when(jnp.logical_and(first, j > turnover))
+        def _():
+            def old(i, carry):
+                finish_far(i)
+                return carry
+
+            lax.fori_loop(jnp.where(j == turnover + 1, 0, j - 1), j, old, 0)
 
         return carry
 

time: 201 us -> 198 us (0.985)
    pallas_call x1, Pallas kernels: 194 us -> 192 us  [local(): pl.pallas_call(functools.partial(kernel, rows_count, full_width), out_sha...]
where the time goes in v4:
time: 198 us; the launch traced here: 195 us
  Pallas kernels  192 us (97%)
  local copies, waits for them, and re-layouts  3.83 us (2%)
    pallas_call x1, Pallas kernels, local(): pl.pallas_call(functools.partial(kernel, rows_count, full_width), out_sha...  192 us

profile of v4, /device:TPU:32, one launch (start us, length us, event | category | flops | bytes accessed | tf_op | source)
XLA Modules:
  0.0 195.4 jit_solution(7008118912728615310)
XLA Ops:
  0.0 1.3 reshape.6.group_ref
  1.3 1.3 reshape.7.code_ref
  2.5 191.6 %shard_map.37 = f32[2,768]{1,0:T(2,128)} custom-call(bf16[768,4096]{1,0:T(8,128)(2,1)} %x_hbm.1, s32[1,768]{1,0:T(1,128)} %reshape.6.group_ref, s32[1,768]{1,0:T(1,128)} %reshape.7.code_ref), custom_call_target="tpu_custom_call" | custom-call | tf_op jit(solution)/shard_map/pallas_call | solution.py:482
  194.1 1.3 copy.5

commit v5 on v4

--- a/solution.py
+++ b/solution.py
@@ -208,7 +208,8 @@
     @pl.when(high)
     def _():
         leg_copy(4).start()
-        fwd_copy(straight[0]).start()
+        for j in straight:
+            fwd_copy(j).start()
 
     send_fwd((1, 2, 3, 4, 5))
     send_back((1, 2, 3, 4, 5))
@@ -313,7 +314,6 @@
 
     def main(j, carry):
         for turn_at, role, act in (
-            (1, high, lambda: fwd_copy(straight[1]).start()),
             (0, side, lambda: pass_on((leg_copy(1), side_copy(1)))),
             (2, side, lambda: pass_on((leg_copy(4), side_copy(4)))),
             (0, next_high, lambda: pass_on((leg_copy(2), row_copy(2)))),

time: 198 us -> 200 us (1.010)
  no operation moved by 1% of the time
where the time goes in v5:
time: 200 us; the launch traced here: 197 us
  Pallas kernels  193 us (96%)
  local copies, waits for them, and re-layouts  3.83 us (2%)
    pallas_call x1, Pallas kernels, local(): pl.pallas_call(functools.partial(kernel, rows_count, full_width), out_sha...  193 us

profile of v5, /device:TPU:32, one launch (start us, length us, event | category | flops | bytes accessed | tf_op | source)
XLA Modules:
  0.0 196.8 jit_solution(16292804913739249212)
XLA Ops:
  0.0 1.3 reshape.6.group_ref
  1.3 1.3 reshape.7.code_ref
  2.5 193.0 %shard_map.37 = f32[2,768]{1,0:T(2,128)} custom-call(bf16[768,4096]{1,0:T(8,128)(2,1)} %x_hbm.1, s32[1,768]{1,0:T(1,128)} %reshape.6.group_ref, s32[1,768]{1,0:T(1,128)} %reshape.7.code_ref), custom_call_target="tpu_custom_call" | custom-call | tf_op jit(solution)/shard_map/pallas_call | solution.py:482
  195.6 1.3 copy.5
